TPU v7x, 32 devices: a whole 2x2x4 slice. The times are simulated.
32 devices in a mesh: dp: 8 (over y, x, core), tensor: 4 (over z).
Axes of the slice: x: 2, y: 2, z: 4, core: 2. Of those that a mesh axis runs over, the one named last changes fastest.
Arguments:
- tokens: bfloat16 [16384, 768], P(('dp', 'tensor')), may hold values from -6 to 6
- starts: int32 [8, 8], P('dp'), may hold values from 0 to 2047, as said below
- w_qkv: bfloat16 [768, 2304], P(None, 'tensor'), may hold values from -0.21875 to 0.21875
- b_qkv: bfloat16 [2304], P('tensor'), may hold values from -3 to 3
- w_out: bfloat16 [768, 768], P('tensor'), may hold values from -2 to 2
- b_out: bfloat16 [768], replicated, may hold values from -3 to 3
- gain_one: bfloat16 [768], replicated, may hold values from 0.099609375 to 1.8984375
- shift_one: bfloat16 [768], replicated, may hold values from -3 to 3
- w_in: bfloat16 [768, 3072], P(None, 'tensor'), may hold values from -0.21875 to 0.21875
- b_in: bfloat16 [3072], P('tensor'), may hold values from -3 to 3
- w_two: bfloat16 [3072, 768], P('tensor'), may hold values from -0.21875 to 0.21875
- b_two: bfloat16 [768], replicated, may hold values from -3 to 3
- gain_two: bfloat16 [768], replicated, may hold values from 0.099609375 to 1.8984375
- shift_two: bfloat16 [768], replicated, may hold values from -3 to 3
- cotangent: bfloat16 [16384, 768], P(('dp', 'tensor')), may hold values from -6 to 6
Outputs:
- block_out: bfloat16 [16384, 768], P(('dp', 'tensor'))
- d_tokens: bfloat16 [16384, 768], P(('dp', 'tensor'))
- d_w_qkv: float32 [768, 2304], P(None, 'tensor')
- d_b_qkv: float32 [2304], P('tensor')
- d_w_out: float32 [768, 768], P('tensor')
- d_b_out: float32 [768], replicated
- d_gain_one: float32 [768], replicated
- d_shift_one: float32 [768], replicated
- d_w_in: float32 [768, 3072], P(None, 'tensor')
- d_b_in: float32 [3072], P('tensor')
- d_w_two: float32 [3072, 768], P('tensor')
- d_b_two: float32 [768], replicated
- d_gain_two: float32 [768], replicated
- d_shift_two: float32 [768], replicated
Inputs may be any that keep to these rules, and one draw needn't show every extreme that they name: Each row holds exactly 8 documents: its first start is 0 and its starts rise strictly. In the first row the last document is a single token.
All inputs are finite; a program needn't handle non-finite values.
Results may differ from a plain program's by a relative error of at most 0.014.
Values may be sent and summed in bfloat16 or wider, within the bound.
No kernel may reach another device: no remote copies, remote signals or barrier semaphores. Data moves between devices by JAX's collectives and lax.ppermute only.
A program may use at most 192 MiB of HBM per device.

v0:
```python
import math
import jax
import jax.numpy as jnp
from jax import lax
from jax.sharding import PartitionSpec as P

HEAD = 64
GROUP = 64
ROW_LEN = 2048
DOCS = 8
highest = lax.Precision.HIGHEST


def doc_tables(starts_row):
    places = jnp.arange(ROW_LEN, dtype=jnp.int32)
    started = (places[:, None] >= starts_row[None, :]).astype(jnp.int32)
    doc_ids = jnp.sum(started, axis=1) - 1
    onehot = (doc_ids[:, None] == jnp.arange(DOCS, dtype=jnp.int32)[None, :]).astype(jnp.int32)
    finish = jnp.concatenate([starts_row[1:], jnp.full((1,), ROW_LEN, jnp.int32)])
    own_start = jnp.sum(onehot * starts_row[None, :], axis=1)
    own_len = jnp.sum(onehot * (finish - starts_row)[None, :], axis=1)
    angles = 0.5 * math.pi * (places - own_start).astype(jnp.float32) / own_len.astype(jnp.float32)
    return (angles, doc_ids)


def attend(mixed, angles, doc_ids):
    length = mixed.shape[0]
    head_count = mixed.shape[1] // (3 * HEAD)
    blocks = length // GROUP
    pieces = mixed.reshape(blocks, GROUP, head_count, 3, HEAD)
    queries = jax.nn.relu(pieces[:, :, :, 0])
    key_pos = jax.nn.relu(pieces[:, :, :, 1])
    values = pieces[:, :, :, 2]
    cosine = jnp.cos(angles).reshape(blocks, GROUP, 1, 1)
    sines = jnp.sin(angles).reshape(blocks, GROUP, 1, 1)
    query_feat = jnp.concatenate([queries * cosine, queries * sines], axis=-1)
    key_feat = jnp.concatenate([key_pos * cosine, key_pos * sines], axis=-1)
    doc_blocks = doc_ids.reshape(blocks, GROUP)
    within = jnp.arange(GROUP, dtype=jnp.int32)
    inside_mask = (
        (doc_blocks[:, :, None] == doc_blocks[:, None, :])
        & (within[None, :, None] >= within[None, None, :])
    ).astype(jnp.float32)
    scores = (
        jnp.einsum("bihf,bjhf->bhij", query_feat, key_feat, precision=highest)
        * inside_mask[:, None]
    )
    numerator = jnp.einsum("bhij,bjhd->bihd", scores, values, precision=highest)
    denominator = jnp.transpose(jnp.sum(scores, axis=-1), (0, 2, 1))
    first_doc = doc_blocks[:, 0]
    last_doc = doc_blocks[:, -1]
    tail_mask = (doc_blocks == last_doc[:, None]).astype(jnp.float32)
    states = jnp.einsum("bjhf,bjhd,bj->bhfd", key_feat, values, tail_mask, precision=highest)
    key_sums = jnp.einsum("bjhf,bj->bhf", key_feat, tail_mask, precision=highest)
    order = jnp.arange(blocks, dtype=jnp.int32)
    link_mask = (
        (last_doc[None, :] == first_doc[:, None]) & (order[None, :] < order[:, None])
    ).astype(jnp.float32)
    carried = jnp.einsum("cb,bhfd->chfd", link_mask, states, precision=highest)
    carried_sum = jnp.einsum("cb,bhf->chf", link_mask, key_sums, precision=highest)
    opening = (doc_blocks == first_doc[:, None]).astype(jnp.float32)
    numerator = numerator + jnp.einsum(
        "bihf,bhfd,bi->bihd", query_feat, carried, opening, precision=highest
    )
    denominator = denominator + jnp.einsum(
        "bihf,bhf,bi->bih", query_feat, carried_sum, opening, precision=highest
    )
    result = numerator / jnp.maximum(denominator, 1.0)[..., None]
    return result.reshape(length, head_count * HEAD)


def attend_rows(mixed, angles, doc_ids):
    row_count = angles.shape[0]
    shaped = mixed.reshape(row_count, angles.shape[1], mixed.shape[1])
    return jax.vmap(attend)(shaped, angles, doc_ids).reshape(mixed.shape[0], -1)


def normalize(rows_in, gain, shift):
    centred = rows_in - jnp.mean(rows_in, axis=-1, keepdims=True)
    spread = jnp.mean(centred * centred, axis=-1, keepdims=True)
    return centred * lax.rsqrt(spread + 1e-05) * gain + shift


def smooth(values):
    return jax.nn.gelu(values)


def inner_rows(left, right):
    return lax.dot_general(
        left, right, (((0,), (0,)), ((), ())), preferred_element_type=jnp.float32
    )


def times_rows(left, right):
    return lax.dot_general(
        left, right, (((1,), (1,)), ((), ())), preferred_element_type=jnp.float32
    )


def rows_product(source, weight):
    return jnp.dot(source, weight, preferred_element_type=jnp.float32)


def rows_back(source, weight):
    return times_rows(source, weight)


def on_device(
    tokens,
    starts,
    w_qkv,
    b_qkv,
    w_out,
    b_out,
    gain_one,
    shift_one,
    w_in,
    b_in,
    w_two,
    b_two,
    gain_two,
    shift_two,
    cotangent,
):
    angles, doc_ids = jax.vmap(doc_tables)(starts)
    bias_qkv = b_qkv.astype(jnp.float32)
    bias_in = b_in.astype(jnp.float32)
    gain_a = gain_one.astype(jnp.float32)
    shift_a = shift_one.astype(jnp.float32)
    gain_b = gain_two.astype(jnp.float32)
    shift_b = shift_two.astype(jnp.float32)
    input_full = lax.all_gather(tokens, "tensor", axis=0, tiled=True)
    mixed = jnp.dot(input_full, w_qkv, preferred_element_type=jnp.float32) + bias_qkv
    attended = attend_rows(mixed, angles, doc_ids).astype(jnp.bfloat16)
    branch = lax.psum_scatter(
        rows_product(attended, w_out), "tensor", scatter_dimension=0, tiled=True
    ) + b_out.astype(jnp.float32)
    first_sum = tokens.astype(jnp.float32) + branch
    first_low = normalize(first_sum, gain_a, shift_a).astype(jnp.bfloat16)
    middle_full = lax.all_gather(first_low, "tensor", axis=0, tiled=True)
    hidden = jnp.dot(middle_full, w_in, preferred_element_type=jnp.float32) + bias_in
    active = smooth(hidden).astype(jnp.bfloat16)
    second = lax.psum_scatter(
        rows_product(active, w_two), "tensor", scatter_dimension=0, tiled=True
    ) + b_two.astype(jnp.float32)
    second_sum = first_low.astype(jnp.float32) + second
    block_out = normalize(second_sum, gain_b, shift_b).astype(jnp.bfloat16)
    input_back = lax.all_gather(tokens, "tensor", axis=0, tiled=True)
    middle_back = lax.all_gather(first_low, "tensor", axis=0, tiled=True)
    unused_two, norm_two_back = jax.vjp(normalize, second_sum, gain_b, shift_b)
    d_r2, d_gain_two, d_shift_two = norm_two_back(cotangent.astype(jnp.float32))
    d_second = d_r2.astype(jnp.bfloat16)
    d_b_two = jnp.sum(d_second, axis=0, dtype=jnp.float32)
    second_full = lax.all_gather(d_second, "tensor", axis=0, tiled=True)
    hidden_again = jnp.dot(middle_back, w_in, preferred_element_type=jnp.float32) + bias_in
    active_val, gelu_back = jax.vjp(smooth, hidden_again)
    active_again = active_val.astype(jnp.bfloat16)
    d_w_two = inner_rows(active_again, second_full)
    d_active = times_rows(second_full, w_two)
    d_hidden = gelu_back(d_active)[0].astype(jnp.bfloat16)
    d_b_in = jnp.sum(d_hidden, axis=0, dtype=jnp.float32)
    d_w_in = inner_rows(middle_back, d_hidden)
    d_first = (
        lax.psum_scatter(rows_back(d_hidden, w_in), "tensor", scatter_dimension=0, tiled=True)
        + d_r2
    )
    unused_one, norm_one_back = jax.vjp(normalize, first_sum, gain_a, shift_a)
    d_r1, d_gain_one, d_shift_one = norm_one_back(d_first)
    d_branch = d_r1.astype(jnp.bfloat16)
    d_b_out = jnp.sum(d_branch, axis=0, dtype=jnp.float32)
    branch_full = lax.all_gather(d_branch, "tensor", axis=0, tiled=True)
    mixed_again = jnp.dot(input_back, w_qkv, preferred_element_type=jnp.float32) + bias_qkv
    attended_val, attend_back = jax.vjp(
        lambda mixed_in: attend_rows(mixed_in, angles, doc_ids), mixed_again
    )
    attended_again = attended_val.astype(jnp.bfloat16)
    d_w_out = inner_rows(attended_again, branch_full)
    d_attended = times_rows(branch_full, w_out)
    d_mixed = attend_back(d_attended)[0].astype(jnp.bfloat16)
    d_b_qkv = jnp.sum(d_mixed, axis=0, dtype=jnp.float32)
    d_w_qkv = inner_rows(input_back, d_mixed)
    d_tokens = (
        lax.psum_scatter(
            rows_back(d_mixed, w_qkv).astype(jnp.bfloat16),
            "tensor",
            scatter_dimension=0,
            tiled=True,
        ).astype(jnp.float32)
        + d_r1
    ).astype(jnp.bfloat16)
    d_w_qkv, d_b_qkv, d_w_out, d_w_in, d_b_in, d_w_two = lax.psum(
        (d_w_qkv, d_b_qkv, d_w_out, d_w_in, d_b_in, d_w_two), "dp"
    )
    d_b_out, d_gain_one, d_shift_one, d_b_two, d_gain_two, d_shift_two = lax.psum(
        (d_b_out, d_gain_one, d_shift_one, d_b_two, d_gain_two, d_shift_two), ("dp", "tensor")
    )
    return (
        block_out,
        d_tokens,
        d_w_qkv,
        d_b_qkv,
        d_w_out,
        d_b_out,
        d_gain_one,
        d_shift_one,
        d_w_in,
        d_b_in,
        d_w_two,
        d_b_two,
        d_gain_two,
        d_shift_two,
    )


def solution(mesh):
    in_specs = (
        P(("dp", "tensor"), None),
        P("dp", None),
        P(None, "tensor"),
        P("tensor"),
        P("tensor", None),
        P(),
        P(),
        P(),
        P(None, "tensor"),
        P("tensor"),
        P("tensor", None),
        P(),
        P(),
        P(),
        P(("dp", "tensor"), None),
    )
    out_specs = (
        P(("dp", "tensor"), None),
        P(("dp", "tensor"), None),
        P(None, "tensor"),
        P("tensor"),
        P("tensor", None),
        P(),
        P(),
        P(),
        P(None, "tensor"),
        P("tensor"),
        P("tensor", None),
        P(),
        P(),
        P(),
    )
    return jax.shard_map(
        on_device, mesh=mesh, in_specs=in_specs, out_specs=out_specs, check_vma=False
    )
```

profile of v0, /device:TPU:0, one launch (start us, length us, event | category | flops | bytes accessed | tf_op | source)
XLA Modules:
  0.0 1038.7 jit_solution(10530214980209661449)
XLA Ops:
  12.7 63.1 %all-gather.5.cloned.1.call-done = bf16[2048,768]{1,0:T(8,128)(2,1)} async-done(((bf16[512,768]{1,0:T(8,128)(2,1)}), bf16[2048,768]{1,0:T(8,128)(2,1)}) %all-gather.5.cloned.1.call-update) | async-done | bytes 3145744 | tf_op jit(solution)/shard_map/all_gather | solution.py:132
  75.8 6.3 convolution_add_fusion
  82.2 8.7 reshape_reshape.3
  90.9 8.2 fusion.101
  110.8 5.1 bitcast_multiply_fusion.4
  123.8 6.0 fusion.31
  134.0 5.0 fusion.78
  139.0 5.4 multiply_reduce_fusion.1
  144.4 5.4 fusion.24
  150.5 9.1 divide_convert_fusion
  169.7 107.1 %reduce-scatter.5.cloned.1.call-done = f32[512,768]{1,0:T(8,128)} async-done(((f32[2048,768]{1,0:T(8,128)}), f32[512,768]{1,0:T(8,128)}) %reduce-scatter.5.cloned.1.call-update) | async-done | bytes 1572880 | tf_op jit(solution)/shard_map/reduce_scatter | solution.py:135
  280.2 64.1 %all-gather.7.cloned.1.call-done = bf16[2048,768]{1,0:T(8,128)(2,1)} async-done(((bf16[512,768]{1,0:T(8,128)(2,1)}), bf16[2048,768]{1,0:T(8,128)(2,1)}) %all-gather.7.cloned.1.call-update) | async-done | bytes 3145744 | tf_op jit(solution)/shard_map/all_gather | solution.py:140
  344.3 8.4 multiply_convert_fusion
  361.3 107.1 %reduce-scatter.7.cloned.1.call-done = f32[512,768]{1,0:T(8,128)} async-done(((f32[2048,768]{1,0:T(8,128)}), f32[512,768]{1,0:T(8,128)}) %reduce-scatter.7.cloned.1.call-update) | async-done | bytes 1572880 | tf_op jit(solution)/shard_map/reduce_scatter | solution.py:143
  476.5 64.1 %all-gather.9.cloned.1.call-done = bf16[2048,768]{1,0:T(8,128)(2,1)} async-done(((bf16[512,768]{1,0:T(8,128)(2,1)}), bf16[2048,768]{1,0:T(8,128)(2,1)}) %all-gather.9.cloned.1.call-update) | async-done | bytes 3145744 | tf_op jit(solution)/shard_map/all_gather | solution.py:154
  540.6 9.8 convert_reduce_fusion.1
  556.7 109.5 %reduce-scatter.9.cloned.1.call-done = f32[512,768]{1,0:T(8,128)} async-done(((f32[2048,768]{1,0:T(8,128)}), f32[512,768]{1,0:T(8,128)}) %reduce-scatter.9.cloned.1.call-update) | async-done | bytes 1572880 | tf_op jit(solution)/shard_map/reduce_scatter | solution.py:164
  673.7 63.5 %all-gather.11.cloned.1.call-done = bf16[2048,768]{1,0:T(8,128)(2,1)} async-done(((bf16[512,768]{1,0:T(8,128)(2,1)}), bf16[2048,768]{1,0:T(8,128)(2,1)}) %all-gather.11.cloned.1.call-update) | async-done | bytes 3145744 | tf_op jit(solution)/shard_map/all_gather | solution.py:171
  742.9 12.0 %fusion.21 = f32[32,3,64,64]{2,3,1,0:T(8,128)} fusion(f32[32,3,64,64]{2,3,1,0:T(8,128)} %copy-done.21, f32[32,64,64]{1,2,0:T(8,128)S(1)} %copy-done.12, f32[1,32,64,3,64]{2,1,4,3,0:T(8,128)} %reshape.798, f32[32,64,3]{1,2,0:T(4,128)S(1)} %copy-done.42), kind=kOutput, calls=%fused_computation.38 | convolution fusion | flops 302776320 | bytes 5267456 | tf_op jit(solution)/shard_map/transpose(jvp(vmap(bhij,bjhd->bihd)))/dot_general | solution.py:48
  754.9 7.4 fusion.19
  764.7 5.4 multiply_reduce_fusion
  777.2 8.3 fusion.42
  789.3 5.8 fusion.30
  795.2 7.7 fusion.13
  802.9 7.0 fusion.38
  814.7 8.1 add_bitcast_fusion
  828.5 7.4 copy.171
  835.9 6.7 convert_element_type.170
  847.0 7.1 fusion.108
  864.5 43.0 %all-reduce.3 = (f32[768]{0:T(1024)}, f32[768]{0:T(1024)}, f32[768]{0:T(1024)}, f32[768]{0:T(1024)}, f32[768]{0:T(1024)}, /*index=5*/f32[768]{0:T(1024)}) all-reduce(f32[768]{0:T(1024)S(1)} %copy-done.71, f32[768]{0:T(1024)S(1)} %copy-done.72, f32[768]{0:T(1024)S(1)} %copy-done.73, ...), channel_id=1, replica_groups=mesh['dp'=8,'tensor'=4] {'dp','tensor'}, use_global_device_ids=true, to_apply=%region_22.23 | all-reduce | flops 4608 | bytes 36864 | tf_op jit(solution)/shard_map/psum | solution.py:194
  907.5 14.0 %all-reduce.4 = (f32[576]{0:T(1024)}, f32[768]{0:T(1024)}) all-reduce(f32[576]{0:T(1024)S(1)} %reduce_sum.223, f32[768]{0:T(1024)S(1)} %copy-done.76), channel_id=1, replica_groups=mesh['dp'=8,'tensor'=4] {'dp'}, use_global_device_ids=true, to_apply=%region_19.20 | all-reduce | flops 1344 | bytes 10752 | tf_op jit(solution)/shard_map/psum | solution.py:191
  923.8 101.3 %all-reduce.8.cloned.1.call-done = (f32[768,576]{0,1:T(8,128)}, f32[192,768]{1,0:T(8,128)}, f32[768,768]{1,0:T(8,128)}, f32[768,768]{1,0:T(8,128)}) async-done(((f32[768,576]{0,1:T(8,128)}, f32[192,768]{1,0:T(8,128)}, f32[768,768]{1,0:T(8,128)}, f32[768,768]{1,0:T(8,128)}), (f32[768,576]{0,1:T(8,128)}, f32[192,768]{1,0:T(8,128)}, f32[768,768]{1,0:T(8,128)}, ...) | async-done | bytes 7077904 | tf_op jit(solution)/shard_map/psum | solution.py:191
  (281 shorter events, 126.3 us)
Async XLA Ops:
  7.2 337.2 %copy-start = (bf16[768,768]{1,0:T(8,128)(2,1)S(1)}, bf16[768,768]{1,0:T(8,128)(2,1)}, u32[]{:S(2)}) copy-start(bf16[768,768]{1,0:T(8,128)(2,1)} %param.23) | copy-start | bytes 3538948
  7.2 68.6 %all-gather.5.cloned.1.call-start = ((), (), s32[]{:S(2)}) async-start(), calls=%async_computation.4 | async-start | bytes 3932160 | tf_op jit(solution)/shard_map/all_gather | solution.py:132
  7.9 268.9 %reduce-scatter.5.cloned.1.call-start = ((), (), s32[]{:S(2)}) async-start(), calls=%async_computation.5 | async-start | bytes 7864320 | tf_op jit(solution)/shard_map/reduce_scatter | solution.py:135
  12.1 117.7 %copy-start.61 = (s32[32]{0:T(128)}, s32[32]{0:T(128)S(1)}, u32[]{:S(2)}) copy-start(s32[32]{0:T(128)S(1)} %get-tuple-element.20) | copy-start | bytes 388
  12.1 117.7 %copy-start.64 = (s32[32]{0:T(128)}, s32[32]{0:T(128)S(1)}, u32[]{:S(2)}) copy-start(s32[32]{0:T(128)S(1)} %get-tuple-element.21) | copy-start | bytes 388
  12.2 109.0 %copy-start.39 = (f32[32,64]{1,0:T(8,128)}, f32[32,64]{1,0:T(8,128)S(1)}, u32[]{:S(2)}) copy-start(f32[32,64]{1,0:T(8,128)S(1)} %get-tuple-element.57) | copy-start | bytes 24580
  12.3 98.5 %copy-start.44 = (f32[32,64]{1,0:T(8,128)}, f32[32,64]{1,0:T(8,128)S(1)}, u32[]{:S(2)}) copy-start(f32[32,64]{1,0:T(8,128)S(1)} %get-tuple-element.71) | copy-start | bytes 24580
  12.3 98.4 %copy-start.46 = (f32[32,64]{1,0:T(8,128)}, f32[32,64]{1,0:T(8,128)S(1)}, u32[]{:S(2)}) copy-start(f32[32,64]{1,0:T(8,128)S(1)} %get-tuple-element.72) | copy-start | bytes 24580
  12.7 131.7 %copy-start.11 = (f32[32,64,64]{1,2,0:T(8,128)}, f32[32,64,64]{1,2,0:T(8,128)S(1)}, u32[]{:S(2)}) copy-start(f32[32,64,64]{1,2,0:T(8,128)S(1)} %and_convert_fusion) | copy-start | bytes 1572868
  167.2 109.6 %copy-start.27 = (bf16[512,768]{1,0:T(8,128)(2,1)S(1)}, bf16[512,768]{1,0:T(8,128)(2,1)}, u32[]{:S(2)}) copy-start(bf16[512,768]{1,0:T(8,128)(2,1)} %param.15) | copy-start | bytes 2359300
  167.3 177.1 %all-gather.7.cloned.1.call-start = ((), (), s32[]{:S(2)}) async-start(), calls=%async_computation.6 | async-start | bytes 3932160 | tf_op jit(solution)/shard_map/all_gather | solution.py:140
  278.6 74.1 %copy-start.50 = (f32[512]{0:T(512)}, f32[512]{0:T(512)S(1)}, u32[]{:S(2)}) copy-start(f32[512]{0:T(512)S(1)} %broadcast_multiply_fusion.1) | copy-start | bytes 6148
  278.9 73.8 %copy-start.57 = (f32[512]{0:T(512)}, f32[512]{0:T(512)S(1)}, u32[]{:S(2)}) copy-start(f32[512]{0:T(512)S(1)} %multiply_reduce_fusion.5) | copy-start | bytes 6148
  278.9 73.8 %copy-start.53 = (f32[512]{0:T(512)}, f32[512]{0:T(512)S(1)}, u32[]{:S(2)}) copy-start(f32[512]{0:T(512)S(1)} %fusion.86) | copy-start | bytes 6148
  280.2 188.3 %reduce-scatter.7.cloned.1.call-start = ((), (), s32[]{:S(2)}) async-start(), calls=%async_computation.7 | async-start | bytes 7864320 | tf_op jit(solution)/shard_map/reduce_scatter | solution.py:143
  280.2 72.5 %copy-start.74 = (f32[768]{0:T(1024)}, f32[768]{0:T(1024)S(1)}, u32[]{:S(2)}) copy-start(f32[768]{0:T(1024)S(1)} %convert_element_type.159) | copy-start | bytes 9220
  358.9 181.8 %all-gather.9.cloned.1.call-start = ((), (), s32[]{:S(2)}) async-start(), calls=%async_computation.8 | async-start | bytes 3932160 | tf_op jit(solution)/shard_map/all_gather | solution.py:154
  361.3 109.5 %copy-start.26 = (bf16[512,768]{1,0:T(8,128)(2,1)S(1)}, bf16[512,768]{1,0:T(8,128)(2,1)}, u32[]{:S(2)}) copy-start(bf16[512,768]{1,0:T(8,128)(2,1)} %param.29) | copy-start | bytes 2359300
  473.6 67.0 %copy-start.75 = (f32[768]{0:T(1024)S(1)}, f32[768]{0:T(1024)}, u32[]{:S(2)}) copy-start(f32[768]{0:T(1024)} %copy-done.74) | copy-start | bytes 9220
  476.4 189.7 %reduce-scatter.9.cloned.1.call-start = ((), (), s32[]{:S(2)}) async-start(), calls=%async_computation.9 | async-start | bytes 7864320 | tf_op jit(solution)/shard_map/reduce_scatter | solution.py:164
  556.6 109.6 %copy-start.49 = (f32[768]{0:T(1024)S(1)}, f32[768]{0:T(1024)}, u32[]{:S(2)}) copy-start(f32[768]{0:T(1024)} %convert_element_type.155) | copy-start | bytes 9220
  556.6 109.6 %copy-start.51 = (f32[512]{0:T(512)S(1)}, f32[512]{0:T(512)}, u32[]{:S(2)}) copy-start(f32[512]{0:T(512)} %copy-done.50) | copy-start | bytes 6148
  556.6 109.6 %copy-start.54 = (f32[512]{0:T(512)S(1)}, f32[512]{0:T(512)}, u32[]{:S(2)}) copy-start(f32[512]{0:T(512)} %copy-done.53) | copy-start | bytes 6148
  556.6 112.9 %copy-start.58 = (f32[512]{0:T(512)S(1)}, f32[512]{0:T(512)}, u32[]{:S(2)}) copy-start(f32[512]{0:T(512)} %copy-done.57) | copy-start | bytes 6148
  556.6 180.5 %all-gather.11.cloned.1.call-start = ((), (), s32[]{:S(2)}) async-start(), calls=%async_computation.10 | async-start | bytes 3932160 | tf_op jit(solution)/shard_map/all_gather | solution.py:171
  669.5 67.7 %copy-start.31 = (bf16[192,768]{1,0:T(8,128)(2,1)S(1)}, bf16[192,768]{1,0:T(8,128)(2,1)}, u32[]{:S(2)}) copy-start(bf16[192,768]{1,0:T(8,128)(2,1)} %param.19) | copy-start | bytes 884740
  670.2 70.1 %copy-start.59 = (f32[512]{0:T(512)}, f32[512]{0:T(512)S(1)}, u32[]{:S(2)}) copy-start(f32[512]{0:T(512)S(1)} %negate_multiply_fusion) | copy-start | bytes 6148
  673.0 248.5 %reduce-scatter.11.cloned.1.call-start = ((), (), s32[]{:S(2)}) async-start(), calls=%async_computation.11 | async-start | bytes 3932160 | tf_op jit(solution)/shard_map/reduce_scatter | solution.py:183
  846.7 178.4 %all-reduce.8.cloned.1.call-start = ((), (), s32[]{:S(2)}) async-start(), calls=%async_computation.12 | async-start | bytes 14155776 | tf_op jit(solution)/shard_map/psum | solution.py:191
  863.7 43.8 %copy-start.76 = (f32[768]{0:T(1024)S(1)}, f32[768]{0:T(1024)}, u32[]{:S(2)}) copy-start(f32[768]{0:T(1024)} %get-tuple-element.40) | copy-start | bytes 9220
  863.7 57.8 %copy-start.16 = (f32[512,768]{1,0:T(8,128)S(1)}, f32[512,768]{1,0:T(8,128)}, u32[]{:S(2)}) copy-start(f32[512,768]{1,0:T(8,128)} %copy-done.15) | copy-start | bytes 4718596
  863.7 57.8 %copy-start.60 = (f32[512]{0:T(512)S(1)}, f32[512]{0:T(512)}, u32[]{:S(2)}) copy-start(f32[512]{0:T(512)} %copy-done.59) | copy-start | bytes 6148
  (68 other events, 355.0 us)
Sparse Core Ops, SparseCore 0:
  9.6 66.1 all-gather.4
  167.4 109.3 reduce-scatter.4
  280.3 64.0 all-gather.6
  359.0 109.3 reduce-scatter.6
  476.6 64.0 all-gather.8
  556.7 109.3 reduce-scatter.8
  673.1 64.0 all-gather.10
  846.8 59.8 reduce-scatter.10
  911.5 113.5 all-reduce.7
where the time goes:
time: 1050 us; the launch traced here: 1040 us
  waiting for transfers between devices  681 us (65%)
  matrix products  166 us (16%)
  local copies, waits for them, and re-layouts  73.7 us (7%)
  blocking collectives  57 us (5%)
  other arithmetic  45.5 us (4%)
  between operations  15.3 us (1%)
    reduce_scatter x1, waiting for transfers between devices, on_device(): lax.psum_scatter(rows_back(d_hidden, w_in), 'tensor', scatter_dimension=0...  109 us
    reduce_scatter x1, waiting for transfers between devices, on_device(): lax.psum_scatter(rows_product(attended, w_out), 'tensor', scatter_dimensi...  107 us
    reduce_scatter x1, waiting for transfers between devices, on_device(): lax.psum_scatter(rows_product(active, w_two), 'tensor', scatter_dimension...  107 us
    psum x1, waiting for transfers between devices, on_device(): lax.psum((d_w_qkv, d_b_qkv, d_w_out, d_w_in, d_b_in, d_w_two), 'dp')  101 us
    all_gather x1, waiting for transfers between devices, on_device(): second_full = lax.all_gather(d_second, 'tensor', axis=0, tiled=True)  64.1 us
    all_gather x1, waiting for transfers between devices, on_device(): middle_full = lax.all_gather(first_low, 'tensor', axis=0, tiled=True)  64.1 us
    all_gather x1, waiting for transfers between devices, on_device(): branch_full = lax.all_gather(d_branch, 'tensor', axis=0, tiled=True)  63.5 us
    all_gather x1, waiting for transfers between devices, on_device(): input_full = lax.all_gather(tokens, 'tensor', axis=0, tiled=True)  63.1 us
  transfers between devices with their start and end apart: 9, of which 8 were waited for; matrix products, arithmetic and copies ran while one was open for 3% of the time, Pallas kernels for 0%

commit v1 on v0

--- a/solution.py
+++ b/solution.py
@@ -9,6 +9,18 @@
 ROW_LEN = 2048
 DOCS = 8
 highest = lax.Precision.HIGHEST
+
+
+def gather_by_bits(shard, axis, dim):
+    ways, here, turn = (lax.axis_size(axis), lax.axis_index(axis), shard.shape[dim])
+    line, have = (shard, 1)
+    while have < ways:
+        line = jnp.concatenate(
+            [line, lax.ppermute(line, axis, [(d, (d - have) % ways) for d in range(ways)])],
+            axis=dim,
+        )
+        have = 2 * have
+    return jnp.roll(line, here * turn, axis=dim)
 
 
 def doc_tables(starts_row):
@@ -137,7 +149,7 @@
     ) + b_out.astype(jnp.float32)
     first_sum = tokens.astype(jnp.float32) + branch
     first_low = normalize(first_sum, gain_a, shift_a).astype(jnp.bfloat16)
-    middle_full = lax.all_gather(first_low, "tensor", axis=0, tiled=True)
+    middle_full = gather_by_bits(first_low, "tensor", 0)
     hidden = jnp.dot(middle_full, w_in, preferred_element_type=jnp.float32) + bias_in
     active = smooth(hidden).astype(jnp.bfloat16)
     second = lax.psum_scatter(

time: 1050 us -> 1140 us (1.086)
  waiting for transfers between devices: 681 us -> 745 us
    ppermute x0 -> x2, waiting for transfers between devices: none -> 81.2 us  [gather_by_bits(): lax.ppermute(line, axis, [(d, (d - have) % ways) for d in range(ways)])]
  transfers between devices with their start and end apart: 9 -> 11, of which waited for: 8 -> 10; matrix products, arithmetic and copies ran while one was open for 3% -> 4% of each run, Pallas kernels for 0% -> 0%
where the time goes in v1:
time: 1140 us; the launch traced here: 1130 us
  waiting for transfers between devices  745 us (65%)
  matrix products  173 us (15%)
  local copies, waits for them, and re-layouts  82.6 us (7%)
  blocking collectives  57.9 us (5%)
  other arithmetic  49.9 us (4%)
  between operations  15.3 us (1%)
    reduce_scatter x1, waiting for transfers between devices, on_device(): lax.psum_scatter(rows_back(d_hidden, w_in), 'tensor', scatter_dimension=0...  109 us
    reduce_scatter x1, waiting for transfers between devices, on_device(): lax.psum_scatter(rows_product(active, w_two), 'tensor', scatter_dimension...  107 us
    reduce_scatter x1, waiting for transfers between devices, on_device(): lax.psum_scatter(rows_product(attended, w_out), 'tensor', scatter_dimensi...  107 us
    psum x1, waiting for transfers between devices, on_device(): lax.psum((d_w_qkv, d_b_qkv, d_w_out, d_w_in, d_b_in, d_w_two), 'dp')  96.9 us
    ppermute x2, waiting for transfers between devices, gather_by_bits(): lax.ppermute(line, axis, [(d, (d - have) % ways) for d in range(ways)])  81.2 us
    all_gather x1, waiting for transfers between devices, on_device(): branch_full = lax.all_gather(d_branch, 'tensor', axis=0, tiled=True)  63.5 us
    all_gather x1, waiting for transfers between devices, on_device(): input_full = lax.all_gather(tokens, 'tensor', axis=0, tiled=True)  63.1 us
    all_gather x1, waiting for transfers between devices, on_device(): middle_back = lax.all_gather(first_low, 'tensor', axis=0, tiled=True)  58.2 us
  transfers between devices with their start and end apart: 11, of which 10 were waited for; matrix products, arithmetic and copies ran while one was open for 4% of the time, Pallas kernels for 0%

profile of v1, /device:TPU:0, one launch (start us, length us, event | category | flops | bytes accessed | tf_op | source)
XLA Modules:
  0.0 1130.4 jit_solution(855860276207121101)
XLA Ops:
  12.7 63.1 %all-gather.5.cloned.1.call-done = bf16[2048,768]{1,0:T(8,128)(2,1)} async-done(((bf16[512,768]{1,0:T(8,128)(2,1)}), bf16[2048,768]{1,0:T(8,128)(2,1)}) %all-gather.5.cloned.1.call-update) | async-done | bytes 3145744 | tf_op jit(solution)/shard_map/all_gather | solution.py:144
  75.8 6.3 convolution_add_fusion
  82.2 8.7 reshape_reshape.3
  90.9 8.1 fusion.124
  123.7 6.0 fusion.41
  144.3 5.4 fusion.32
  150.5 9.1 divide_convert_fusion
  169.7 107.1 %reduce-scatter.5.cloned.1.call-done = f32[512,768]{1,0:T(8,128)} async-done(((f32[2048,768]{1,0:T(8,128)}), f32[512,768]{1,0:T(8,128)}) %reduce-scatter.5.cloned.1.call-update) | async-done | bytes 1572880 | tf_op jit(solution)/shard_map/reduce_scatter | solution.py:147
  283.3 17.0 %collective-permute-done = bf16[512,768]{1,0:T(8,128)(2,1)S(1)} collective-permute-done((bf16[512,768]{1,0:T(8,128)(2,1)S(1)}, bf16[512,768]{1,0:T(8,128)(2,1)S(1)}, u32[]{:S(2)}, u32[]{:S(2)}) %collective-permute-start) | collective-permute-done | bytes 786464 | tf_op jit(solution)/shard_map/ppermute | solution.py:19
  308.6 64.2 %collective-permute-done.1 = bf16[1024,768]{1,0:T(8,128)(2,1)} collective-permute-done((bf16[1024,768]{1,0:T(8,128)(2,1)}, bf16[1024,768]{1,0:T(8,128)(2,1)}, u32[]{:S(2)}, u32[]{:S(2)}) %collective-permute-start.1) | collective-permute-done | bytes 1572896 | tf_op jit(solution)/shard_map/ppermute | solution.py:19
  380.2 9.4 fusion.79
  394.0 107.5 %reduce-scatter.7.cloned.1.call-done = f32[512,768]{1,0:T(8,128)} async-done(((f32[2048,768]{1,0:T(8,128)}), f32[512,768]{1,0:T(8,128)}) %reduce-scatter.7.cloned.1.call-update) | async-done | bytes 1572880 | tf_op jit(solution)/shard_map/reduce_scatter | solution.py:155
  509.4 58.2 %all-gather.9.cloned.1.call-done = bf16[2048,768]{1,0:T(8,128)(2,1)} async-done(((bf16[512,768]{1,0:T(8,128)(2,1)}), bf16[2048,768]{1,0:T(8,128)(2,1)}) %all-gather.9.cloned.1.call-update) | async-done | bytes 3145744 | tf_op jit(solution)/shard_map/all_gather | solution.py:161
  567.6 7.2 fusion.126
  574.7 57.0 %all-gather.7.cloned.1.call-done = bf16[2048,768]{1,0:T(8,128)(2,1)} async-done(((bf16[512,768]{1,0:T(8,128)(2,1)}), bf16[2048,768]{1,0:T(8,128)(2,1)}) %all-gather.7.cloned.1.call-update) | async-done | bytes 3145744 | tf_op jit(solution)/shard_map/all_gather | solution.py:166
  631.7 9.8 convert_reduce_fusion.1
  647.8 109.5 %reduce-scatter.9.cloned.1.call-done = f32[512,768]{1,0:T(8,128)} async-done(((f32[2048,768]{1,0:T(8,128)}), f32[512,768]{1,0:T(8,128)}) %reduce-scatter.9.cloned.1.call-update) | async-done | bytes 1572880 | tf_op jit(solution)/shard_map/reduce_scatter | solution.py:176
  764.9 63.5 %all-gather.11.cloned.1.call-done = bf16[2048,768]{1,0:T(8,128)(2,1)} async-done(((bf16[512,768]{1,0:T(8,128)(2,1)}), bf16[2048,768]{1,0:T(8,128)(2,1)}) %all-gather.11.cloned.1.call-update) | async-done | bytes 3145744 | tf_op jit(solution)/shard_map/all_gather | solution.py:183
  834.1 12.0 %fusion.29 = f32[32,3,64,64]{2,3,1,0:T(8,128)} fusion(f32[32,3,64,64]{2,3,1,0:T(8,128)} %copy-done.23, f32[32,64,64]{1,2,0:T(8,128)S(1)} %copy-done.12, f32[1,32,64,3,64]{2,1,4,3,0:T(8,128)} %reshape.798, f32[32,64,3]{1,2,0:T(4,128)S(1)} %copy-done.46), kind=kOutput, calls=%fused_computation.47 | convolution fusion | flops 302776320 | bytes 5267456 | tf_op jit(solution)/shard_map/transpose(jvp(vmap(bhij,bjhd->bihd)))/dot_general | solution.py:60
  846.1 7.4 fusion.27
  868.4 8.3 fusion.52
  880.5 5.8 fusion.40
  886.4 7.7 fusion.21
  894.1 7.1 fusion.48
  906.0 8.1 add_bitcast_fusion
  919.8 7.4 copy.171
  927.3 6.7 convert_element_type.172
  938.5 7.1 fusion.130
  945.6 7.9 fusion.39
  959.6 43.6 %all-reduce.3 = (f32[768]{0:T(1024)}, f32[768]{0:T(1024)}, f32[768]{0:T(1024)}, f32[768]{0:T(1024)}, f32[768]{0:T(1024)}, /*index=5*/f32[768]{0:T(1024)}) all-reduce(f32[768]{0:T(1024)S(1)} %copy-done.75, f32[768]{0:T(1024)S(1)} %copy-done.76, f32[768]{0:T(1024)S(1)} %copy-done.77, ...), channel_id=1, replica_groups=mesh['dp'=8,'tensor'=4] {'dp','tensor'}, use_global_device_ids=true, to_apply=%region_22.23 | all-reduce | flops 4608 | bytes 36864 | tf_op jit(solution)/shard_map/psum | solution.py:206
  1003.3 14.3 %all-reduce.4 = (f32[576]{0:T(1024)}, f32[768]{0:T(1024)}) all-reduce(f32[576]{0:T(1024)S(1)} %reduce_sum.223, f32[768]{0:T(1024)S(1)} %copy-done.81), channel_id=1, replica_groups=mesh['dp'=8,'tensor'=4] {'dp'}, use_global_device_ids=true, to_apply=%region_19.20 | all-reduce | flops 1344 | bytes 10752 | tf_op jit(solution)/shard_map/psum | solution.py:203
  1019.9 96.9 %all-reduce.8.cloned.1.call-done = (f32[768,576]{0,1:T(8,128)}, f32[192,768]{1,0:T(8,128)}, f32[768,768]{1,0:T(8,128)}, f32[768,768]{1,0:T(8,128)}) async-done(((f32[768,576]{0,1:T(8,128)}, f32[192,768]{1,0:T(8,128)}, f32[768,768]{1,0:T(8,128)}, f32[768,768]{1,0:T(8,128)}), (f32[768,576]{0,1:T(8,128)}, f32[192,768]{1,0:T(8,128)}, f32[768,768]{1,0:T(8,128)}, ...) | async-done | bytes 7077904 | tf_op jit(solution)/shard_map/psum | solution.py:203
  (287 shorter events, 157.5 us)
Async XLA Ops:
  7.2 373.0 %copy-start = (bf16[768,768]{1,0:T(8,128)(2,1)S(1)}, bf16[768,768]{1,0:T(8,128)(2,1)}, u32[]{:S(2)}) copy-start(bf16[768,768]{1,0:T(8,128)(2,1)} %param.23) | copy-start | bytes 3538948
  7.2 68.6 %all-gather.5.cloned.1.call-start = ((), (), s32[]{:S(2)}) async-start(), calls=%async_computation.4 | async-start | bytes 3932160 | tf_op jit(solution)/shard_map/all_gather | solution.py:144
  7.9 268.9 %reduce-scatter.5.cloned.1.call-start = ((), (), s32[]{:S(2)}) async-start(), calls=%async_computation.5 | async-start | bytes 7864320 | tf_op jit(solution)/shard_map/reduce_scatter | solution.py:147
  12.1 117.6 %copy-start.64 = (s32[32]{0:T(128)}, s32[32]{0:T(128)S(1)}, u32[]{:S(2)}) copy-start(s32[32]{0:T(128)S(1)} %get-tuple-element.20) | copy-start | bytes 388
  12.1 117.6 %copy-start.67 = (s32[32]{0:T(128)}, s32[32]{0:T(128)S(1)}, u32[]{:S(2)}) copy-start(s32[32]{0:T(128)S(1)} %get-tuple-element.21) | copy-start | bytes 388
  12.2 108.9 %copy-start.43 = (f32[32,64]{1,0:T(8,128)}, f32[32,64]{1,0:T(8,128)S(1)}, u32[]{:S(2)}) copy-start(f32[32,64]{1,0:T(8,128)S(1)} %get-tuple-element.59) | copy-start | bytes 24580
  12.3 98.4 %copy-start.48 = (f32[32,64]{1,0:T(8,128)}, f32[32,64]{1,0:T(8,128)S(1)}, u32[]{:S(2)}) copy-start(f32[32,64]{1,0:T(8,128)S(1)} %get-tuple-element.73) | copy-start | bytes 24580
  12.3 98.4 %copy-start.50 = (f32[32,64]{1,0:T(8,128)}, f32[32,64]{1,0:T(8,128)S(1)}, u32[]{:S(2)}) copy-start(f32[32,64]{1,0:T(8,128)S(1)} %get-tuple-element.74) | copy-start | bytes 24580
  12.7 131.6 %copy-start.11 = (f32[32,64,64]{1,2,0:T(8,128)}, f32[32,64,64]{1,2,0:T(8,128)S(1)}, u32[]{:S(2)}) copy-start(f32[32,64,64]{1,2,0:T(8,128)S(1)} %and_convert_fusion) | copy-start | bytes 1572868
  167.2 109.6 %copy-start.31 = (bf16[512,768]{1,0:T(8,128)(2,1)S(1)}, bf16[512,768]{1,0:T(8,128)(2,1)}, u32[]{:S(2)}) copy-start(bf16[512,768]{1,0:T(8,128)(2,1)} %param.15) | copy-start | bytes 2359300
  167.2 334.3 %reduce-scatter.7.cloned.1.call-start = ((), (), s32[]{:S(2)}) async-start(), calls=%async_computation.6 | async-start | bytes 7864320 | tf_op jit(solution)/shard_map/reduce_scatter | solution.py:155
  280.7 94.8 %copy-start.14 = (bf16[512,768]{1,0:T(8,128)(2,1)}, bf16[512,768]{1,0:T(8,128)(2,1)S(1)}, u32[]{:S(2)}) copy-start(bf16[512,768]{1,0:T(8,128)(2,1)S(1)} %get-tuple-element.56) | copy-start | bytes 2359300
  280.7 19.6 %collective-permute-start = (bf16[512,768]{1,0:T(8,128)(2,1)S(1)}, bf16[512,768]{1,0:T(8,128)(2,1)S(1)}, u32[]{:S(2)}, u32[]{:S(2)}) collective-permute-start(bf16[512,768]{1,0:T(8,128)(2,1)S(1)} %get-tuple-element.56), channel_id=1, source_target_pairs={{0,3},{1,0},{2,1},{3,2},{4,7},{5,4},{6,5},{7,6},{8,11},{9,8},{10,9... | collective-permute-start | bytes 2359304 | tf_op jit(solution)/shard_map/ppermute | solution.py:19
  302.4 70.4 %collective-permute-start.1 = (bf16[1024,768]{1,0:T(8,128)(2,1)}, bf16[1024,768]{1,0:T(8,128)(2,1)}, u32[]{:S(2)}, u32[]{:S(2)}) collective-permute-start(bf16[1024,768]{1,0:T(8,128)(2,1)} %pad_maximum_fusion), channel_id=1, source_target_pairs={{0,2},{1,3},{2,0},{3,1},{4,6},{5,7},{6,4},{7,5},{8,10},{9,11},{10,... | collective-permute-start | bytes 4718600 | tf_op jit(solution)/shard_map/ppermute | solution.py:19
  306.3 70.1 %copy-start.28 = (bf16[512,768]{1,0:T(8,128)(2,1)S(1)}, bf16[512,768]{1,0:T(8,128)(2,1)}, u32[]{:S(2)}) copy-start(bf16[512,768]{1,0:T(8,128)(2,1)} %copy-done.27) | copy-start | bytes 2359300
  389.5 112.0 %copy-start.15 = (bf16[512,768]{1,0:T(8,128)(2,1)S(1)}, bf16[512,768]{1,0:T(8,128)(2,1)}, u32[]{:S(2)}) copy-start(bf16[512,768]{1,0:T(8,128)(2,1)} %copy-done.14) | copy-start | bytes 2359300
  389.6 178.0 %all-gather.9.cloned.1.call-start = ((), (), s32[]{:S(2)}) async-start(), calls=%async_computation.8 | async-start | bytes 3932160 | tf_op jit(solution)/shard_map/all_gather | solution.py:161
  390.2 241.6 %all-gather.7.cloned.1.call-start = ((), (), s32[]{:S(2)}) async-start(), calls=%async_computation.7 | async-start | bytes 3932160 | tf_op jit(solution)/shard_map/all_gather | solution.py:166
  509.3 122.4 %copy-start.79 = (f32[768]{0:T(1024)S(1)}, f32[768]{0:T(1024)}, u32[]{:S(2)}) copy-start(f32[768]{0:T(1024)} %convert_element_type.161) | copy-start | bytes 9220
  509.3 248.0 %reduce-scatter.9.cloned.1.call-start = ((), (), s32[]{:S(2)}) async-start(), calls=%async_computation.9 | async-start | bytes 7864320 | tf_op jit(solution)/shard_map/reduce_scatter | solution.py:176
  647.7 109.6 %copy-start.54 = (f32[768]{0:T(1024)S(1)}, f32[768]{0:T(1024)}, u32[]{:S(2)}) copy-start(f32[768]{0:T(1024)} %convert_element_type.157) | copy-start | bytes 9220
  647.7 109.6 %copy-start.56 = (f32[512]{0:T(512)S(1)}, f32[512]{0:T(512)}, u32[]{:S(2)}) copy-start(f32[512]{0:T(512)} %copy-done.55) | copy-start | bytes 6148
  647.7 109.6 %copy-start.59 = (f32[512]{0:T(512)S(1)}, f32[512]{0:T(512)}, u32[]{:S(2)}) copy-start(f32[512]{0:T(512)} %copy-done.58) | copy-start | bytes 6148
  647.7 112.9 %copy-start.61 = (f32[512]{0:T(512)S(1)}, f32[512]{0:T(512)}, u32[]{:S(2)}) copy-start(f32[512]{0:T(512)} %copy-done.60) | copy-start | bytes 6148
  647.7 180.6 %all-gather.11.cloned.1.call-start = ((), (), s32[]{:S(2)}) async-start(), calls=%async_computation.10 | async-start | bytes 3932160 | tf_op jit(solution)/shard_map/all_gather | solution.py:183
  760.6 67.7 %copy-start.35 = (bf16[192,768]{1,0:T(8,128)(2,1)S(1)}, bf16[192,768]{1,0:T(8,128)(2,1)}, u32[]{:S(2)}) copy-start(bf16[192,768]{1,0:T(8,128)(2,1)} %param.19) | copy-start | bytes 884740
  761.3 70.1 %copy-start.62 = (f32[512]{0:T(512)}, f32[512]{0:T(512)S(1)}, u32[]{:S(2)}) copy-start(f32[512]{0:T(512)S(1)} %negate_multiply_fusion) | copy-start | bytes 6148
  764.1 253.5 %reduce-scatter.11.cloned.1.call-start = ((), (), s32[]{:S(2)}) async-start(), calls=%async_computation.11 | async-start | bytes 3932160 | tf_op jit(solution)/shard_map/reduce_scatter | solution.py:195
  938.2 178.6 %all-reduce.8.cloned.1.call-start = ((), (), s32[]{:S(2)}) async-start(), calls=%async_computation.12 | async-start | bytes 14155776 | tf_op jit(solution)/shard_map/psum | solution.py:203
  958.9 44.4 %copy-start.81 = (f32[768]{0:T(1024)S(1)}, f32[768]{0:T(1024)}, u32[]{:S(2)}) copy-start(f32[768]{0:T(1024)} %get-tuple-element.40) | copy-start | bytes 9220
  958.9 58.7 %copy-start.18 = (f32[512,768]{1,0:T(8,128)S(1)}, f32[512,768]{1,0:T(8,128)}, u32[]{:S(2)}) copy-start(f32[512,768]{1,0:T(8,128)} %copy-done.17) | copy-start | bytes 4718596
  958.9 58.7 %copy-start.63 = (f32[512]{0:T(512)S(1)}, f32[512]{0:T(512)}, u32[]{:S(2)}) copy-start(f32[512]{0:T(512)} %copy-done.62) | copy-start | bytes 6148
  (68 other events, 359.0 us)
Sparse Core Ops, SparseCore 0:
  9.6 66.1 all-gather.4
  167.4 109.3 reduce-scatter.4
  389.7 111.7 reduce-scatter.6
  503.5 64.0 all-gather.8
  569.5 62.1 all-gather.6
  647.8 109.3 reduce-scatter.8
  764.3 64.0 all-gather.10
  938.3 59.9 reduce-scatter.10
  1003.1 113.6 all-reduce.7
